TPU v7x, 32 devices: a whole 2x2x4 slice. The times are simulated.
32 devices in a mesh: dp: 8 (over y, x, core), mp: 4 (over z).
Axes of the slice: x: 2, y: 2, z: 4, core: 2. Of those that a mesh axis runs over, the one named last changes fastest.
Arguments:
- tokens_in: bfloat16 [1024, 5120], P('dp'), may hold values from -6 to 6
- cotangent: bfloat16 [1024, 10240], P('dp', 'mp'), may hold values from -6 to 6
- old_weights: bfloat16 [112, 128, 128], P('mp'), may hold values from -0.25 to 0.25
- old_first: float32 [112, 16384], P('mp', 'dp'), may hold values from -6 to 6
- old_second: float32 [112, 16384], P('mp', 'dp'), may hold values from 0.25 to 4
- new_coords: int32 [80, 2], replicated, may hold values from 0 to 79, as said below
- moved_to: int32 [112], replicated, may hold values from -1 to 79, as said below
Outputs:
- activated: bfloat16 [1024, 10240], P('dp', 'mp')
- input_grads: bfloat16 [1024, 5120], P('dp', 'mp')
- new_weights: bfloat16 [80, 128, 128], P('mp')
- new_first: float32 [80, 16384], P('mp', 'dp')
- new_second: float32 [80, 16384], P('mp', 'dp')
Inputs may be any that keep to these rules, and one draw needn't show every extreme that they name: new_coords[b] is (row block, column block) of new slot b, owned by mp index b // 20; no two slots share a cell. Call the column blocks of one index of mp a band; no owner has more than 11 blocks in one band, and in every draw some band holds exactly 11 blocks of every owner. moved_to[o] is the new slot that old slot o (held by mp index o // 28) moves to, or -1 where the old block is pruned or the slot is empty. Each new slot is named at most once; new slots that no old slot names are regrown. At most 7 blocks move from one old owner to one new owner; in every draw every new owner receives exactly 7 from some old owner, and some new owner receives 20 blocks in all.
All inputs are finite; a program needn't handle non-finite values.
Results may differ from a plain program's by a relative error of at most 0.0055.
Values may be sent and summed in bfloat16 or wider, within the bound.
No kernel may reach another device: no remote copies, remote signals or barrier semaphores. Data moves between devices by JAX's collectives and lax.ppermute only.
A program may use at most 64 MiB of HBM per device.

v0:
```python
import math
import jax
import jax.numpy as jnp
from jax import lax
from jax.sharding import PartitionSpec as P

BETA_ONE = 0.9
BETA_TWO = 0.95
LEARN_RATE = 0.01
ADAM_EPSILON = 0.05


def gelu_tanh(values):
    return jax.nn.gelu(values, approximate=True)


def pick_rows(source_rows, row_index, filled):
    picked = jnp.take(source_rows, row_index, axis=0)
    shape_tail = (1,) * (source_rows.ndim - 1)
    return jnp.where(filled.reshape((-1,) + shape_tail), picked, jnp.zeros_like(picked))


def inverse_slots(positions, slot_count):
    targets = jnp.arange(slot_count, dtype=jnp.int32)
    matches = positions[None, :] == targets[:, None]
    entries = jnp.arange(positions.shape[0], dtype=jnp.int32)
    source = jnp.sum(jnp.where(matches, entries[None, :], 0), axis=1)
    return (source, jnp.any(matches, axis=1))


def ranks_within(labels, label_count):
    onehot = (labels[:, :, None] == jnp.arange(label_count, dtype=jnp.int32)[None, None, :]).astype(
        jnp.int32
    )
    before = jnp.cumsum(onehot, axis=1) - onehot
    return jnp.sum(before * onehot, axis=2)


def body(tokens_in, cotangent, old_weights, old_first, old_second, new_coords, moved_to):
    owners = lax.axis_size("mp")
    replicas = lax.axis_size("dp")
    owner_here = lax.axis_index("mp")
    replica = lax.axis_index("dp")
    capacity = old_weights.shape[0]
    block_size = old_weights.shape[1]
    total_blocks = new_coords.shape[0]
    per_owner = total_blocks // owners
    shard_len = old_first.shape[1]
    token_count = tokens_in.shape[0]
    model_width = tokens_in.shape[1]
    band_width = cotangent.shape[1] // block_size
    move_slots = capacity // owners
    band_slots = 2 * per_owner // owners + 1
    dest_slot = moved_to.reshape(owners, capacity)
    dest_owner = jnp.where(dest_slot >= 0, dest_slot // per_owner, -1)
    move_rank = ranks_within(dest_owner, owners)
    here_owner = lax.dynamic_index_in_dim(dest_owner, owner_here, 0, keepdims=False)
    here_rank = lax.dynamic_index_in_dim(move_rank, owner_here, 0, keepdims=False)
    send_place = jnp.where(
        here_owner >= 0, here_owner * move_slots + here_rank, owners * move_slots
    )
    send_source, send_filled = inverse_slots(send_place, owners * move_slots)
    outgoing = pick_rows(old_weights, send_source, send_filled)
    out_first = pick_rows(old_first, send_source, send_filled)
    out_second = pick_rows(old_second, send_source, send_filled)
    arrived_weights = lax.all_to_all(outgoing, "mp", split_axis=0, concat_axis=0, tiled=True)
    arrived_first, arrived_second = (
        lax.all_to_all(out_first, "mp", split_axis=0, concat_axis=0, tiled=True),
        lax.all_to_all(out_second, "mp", split_axis=0, concat_axis=0, tiled=True),
    )
    old_owner = jnp.arange(owners * capacity, dtype=jnp.int32) // capacity
    flat_place = old_owner * move_slots + move_rank.reshape(-1)
    recv_source, recv_filled = inverse_slots(moved_to - owner_here * per_owner, per_owner)
    recv_index = jnp.take(flat_place, recv_source)
    weights_now = pick_rows(arrived_weights, recv_index, recv_filled)
    first_now = pick_rows(arrived_first, recv_index, recv_filled)
    second_now = pick_rows(arrived_second, recv_index, recv_filled)
    my_coords = lax.dynamic_slice_in_dim(new_coords, owner_here * per_owner, per_owner, 0)
    row_ids = my_coords[:, 0]
    token_blocks = jnp.take(
        tokens_in.reshape(token_count, model_width // block_size, block_size), row_ids, axis=1
    )
    products = jnp.einsum(
        "tbk,bkn->btn", token_blocks, weights_now, preferred_element_type=jnp.float32
    ).astype(jnp.bfloat16)
    all_band = new_coords[:, 1] // band_width
    band_rank = ranks_within(all_band.reshape(owners, per_owner), owners).reshape(-1)
    my_band = lax.dynamic_slice_in_dim(all_band, owner_here * per_owner, per_owner, 0)
    my_rank = lax.dynamic_slice_in_dim(band_rank, owner_here * per_owner, per_owner, 0)
    out_place = my_band * band_slots + my_rank
    out_source, out_filled = inverse_slots(out_place, owners * band_slots)
    outgoing_products = pick_rows(products, out_source, out_filled)
    arrived_products = lax.all_to_all(
        outgoing_products, "mp", split_axis=0, concat_axis=0, tiled=True
    )
    all_owner = jnp.arange(total_blocks, dtype=jnp.int32) // per_owner
    incoming_key = jnp.where(all_band == owner_here, all_owner * band_slots + band_rank, -1)
    local_col = new_coords[:, 1] - owner_here * band_width
    key_match = (
        incoming_key[None, :] == jnp.arange(owners * band_slots, dtype=jnp.int32)[:, None]
    ).astype(jnp.float32)
    col_match = (local_col[:, None] == jnp.arange(band_width, dtype=jnp.int32)[None, :]).astype(
        jnp.float32
    )
    placement = jnp.dot(key_match, col_match).astype(jnp.bfloat16)
    hidden = jnp.einsum(
        "qc,qtn->tcn", placement, arrived_products, preferred_element_type=jnp.float32
    )
    hidden = hidden.reshape(token_count, band_width * block_size)
    activated = gelu_tanh(hidden).astype(jnp.bfloat16)
    pullback = jax.vjp(gelu_tanh, hidden)[1]
    slopes = pullback(cotangent.astype(jnp.float32))[0].astype(jnp.bfloat16)
    band_slopes = slopes.reshape(token_count, band_width, block_size)
    outgoing_slopes = jnp.einsum(
        "qc,tcn->qtn", placement, band_slopes, preferred_element_type=jnp.float32
    ).astype(jnp.bfloat16)
    arrived_slopes = lax.all_to_all(outgoing_slopes, "mp", split_axis=0, concat_axis=0, tiled=True)
    slope_blocks = jnp.take(arrived_slopes, out_place, axis=0)
    slope_form = "btn"
    block_grads = jnp.einsum(
        "tbk," + slope_form + "->bkn",
        token_blocks,
        slope_blocks,
        preferred_element_type=jnp.float32,
    )
    back_terms = jnp.einsum(
        slope_form + ",bkn->tbk", slope_blocks, weights_now, preferred_element_type=jnp.float32
    )
    input_terms = jnp.zeros((token_count, model_width // block_size, block_size), jnp.float32)
    input_terms = input_terms.at[:, row_ids, :].add(back_terms)
    input_terms = input_terms.reshape(token_count, model_width)
    grad_inputs = lax.psum_scatter(input_terms, "mp", scatter_dimension=1, tiled=True).astype(
        jnp.bfloat16
    )
    flat_grads = block_grads.reshape(per_owner, block_size * block_size)
    summed = lax.psum(flat_grads.astype(jnp.bfloat16), "dp").astype(jnp.float32)
    grad_share = lax.dynamic_slice_in_dim(summed, replica * shard_len, shard_len, 1)
    grad_share = grad_share * (1.0 / math.sqrt(token_count * replicas))
    first_new = BETA_ONE * first_now + (1.0 - BETA_ONE) * grad_share
    second_new = BETA_TWO * second_now + (1.0 - BETA_TWO) * grad_share * grad_share
    flat_weights = weights_now.reshape(per_owner, block_size * block_size)
    weight_share = lax.dynamic_slice_in_dim(flat_weights, replica * shard_len, shard_len, 1).astype(
        jnp.float32
    )
    weight_next = (
        weight_share - LEARN_RATE * first_new / (jnp.sqrt(second_new) + ADAM_EPSILON)
    ).astype(jnp.bfloat16)
    weights_out = lax.all_gather(weight_next, "dp", axis=1, tiled=True).reshape(
        per_owner, block_size, block_size
    )
    return (activated, grad_inputs, weights_out, first_new, second_new)


def solution(mesh):
    in_specs = (
        P("dp", None),
        P("dp", "mp"),
        P("mp", None, None),
        P("mp", "dp"),
        P("mp", "dp"),
        P(),
        P(),
    )
    out_specs = (P("dp", "mp"), P("dp", "mp"), P("mp", None, None), P("mp", "dp"), P("mp", "dp"))
    return jax.shard_map(body, mesh=mesh, in_specs=in_specs, out_specs=out_specs, check_vma=False)
```

profile of v0, /device:TPU:0, one launch (start us, length us, event | category | flops | bytes accessed | tf_op | source)
XLA Modules:
  0.0 213.0 jit_solution(905694268786100202)
XLA Ops:
  8.0 0.7 compare_and_fusion.3
  8.8 0.7 broadcast_subtract_fusion
  9.9 0.2 select_reduce_fusion
  10.4 0.7 gather_fusion.2
  11.2 1.2 select_select_fusion.1
  12.3 6.5 %all-to-all-start = ((bf16[28,128,128]{2,1,0:T(8,128)(2,1)}), bf16[28,128,128]{2,1,0:T(8,128)(2,1)}, u32[]{:S(2)}, u32[]{:S(2)}) async-start(bf16[28,128,128]{2,1,0:T(8,128)(2,1)} %select_select_fusion.1), calls=%async_computation | async-start | bytes 1835008 | tf_op jit(solution)/shard_map/all_to_all | solution.py:66
  19.1 0.5 broadcast.521
  19.6 1.2 fusion.51
  21.2 0.2 select_reduce_fusion.1
  21.5 0.5 compare_select_fusion.10
  22.0 0.7 compare_and_fusion
  22.7 0.6 select_reduce_fusion.4
  23.3 0.7 gather_fusion.1
  24.0 0.5 fusion.40
  24.5 0.8 copy.47
  25.3 0.8 copy.48
  26.2 1.5 gather_fusion
  28.0 0.6 compare_and_fusion.2
  28.6 13.3 %all-to-all-done = bf16[28,128,128]{2,1,0:T(8,128)(2,1)} async-done(((bf16[28,128,128]{2,1,0:T(8,128)(2,1)}), bf16[28,128,128]{2,1,0:T(8,128)(2,1)}, u32[]{:S(2)}, u32[]{:S(2)}) %all-to-all-start) | async-done | bytes 917536 | tf_op jit(solution)/shard_map/all_to_all | solution.py:66
  41.9 1.8 gather_fusion.3
  43.7 0.8 copy-done.3
  44.6 0.4 convolution_convert_fusion.2
  45.0 0.8 gather_fusion.4
  45.8 1.4 select_select_fusion
  47.2 3.5 %all-to-all-start.1 = ((bf16[44,128,128]{2,1,0:T(8,128)(2,1)}), bf16[44,128,128]{2,1,0:T(8,128)(2,1)S(1)}, u32[]{:S(2)}, u32[]{:S(2)}) async-start(bf16[44,128,128]{2,1,0:T(8,128)(2,1)} %select_select_fusion), calls=%async_computation.1 | async-start | bytes 2883584 | tf_op jit(solution)/shard_map/all_to_all | solution.py:93
  50.7 1.4 copy.51
  52.2 0.2 fusion.16
  52.4 32.0 %all-to-all-done.1 = bf16[44,128,128]{2,1,0:T(8,128)(2,1)S(1)} async-done(((bf16[44,128,128]{2,1,0:T(8,128)(2,1)}), bf16[44,128,128]{2,1,0:T(8,128)(2,1)S(1)}, u32[]{:S(2)}, u32[]{:S(2)}) %all-to-all-start.1) | async-done | bytes 1441824 | tf_op jit(solution)/shard_map/all_to_all | solution.py:93
  84.4 2.1 fusion.2
  86.5 1.8 copy.50
  88.3 1.9 fusion.7
  90.2 0.4 copy.52
  90.6 0.6 convolution_convert_fusion
  91.2 1.5 copy.53
  92.7 3.7 %all-to-all-start.2 = ((bf16[44,128,128]{2,1,0:T(8,128)(2,1)}), bf16[44,128,128]{2,1,0:T(8,128)(2,1)S(1)}, u32[]{:S(2)}, u32[]{:S(2)}) async-start(bf16[44,128,128]{2,1,0:T(8,128)(2,1)} %copy.53), calls=%async_computation.2 | async-start | bytes 2883584 | tf_op jit(solution)/shard_map/all_to_all | solution.py:117
  96.5 33.6 %all-to-all-done.2 = bf16[44,128,128]{2,1,0:T(8,128)(2,1)S(1)} async-done(((bf16[44,128,128]{2,1,0:T(8,128)(2,1)}), bf16[44,128,128]{2,1,0:T(8,128)(2,1)S(1)}, u32[]{:S(2)}, u32[]{:S(2)}) %all-to-all-start.2) | async-done | bytes 1441824 | tf_op jit(solution)/shard_map/all_to_all | solution.py:117
  130.0 1.5 gather_fusion.5
  131.6 1.6 convolution_convert_fusion.1
  133.2 1.4 copy.60
  134.7 1.7 fusion.19
  136.5 0.3 broadcast_in_dim.224
  136.8 4.4 %scatter_fusion = f32[128,40,128]{2,0,1:T(8,128)S(1)} fusion(f32[128,40,128]{2,0,1:T(8,128)S(1)} %broadcast_in_dim.224, s32[20]{0:T(128)S(1)} %get-tuple-element.48, f32[20,128,128]{2,1,0:T(8,128)} %fusion.19), kind=kCustom, calls=%fused_computation.10 | custom fusion | flops 327680 | bytes 3932240 | tf_op jit(solution)/shard_map/scatter-add | solution.py:130
  141.2 2.1 copy.54
  143.3 0.6 copy-done.31
  143.9 0.3 copy-done.1
  144.2 0.6 gather_fusion.8
  144.9 0.6 gather_fusion.6
  145.7 0.7 all_to_all.31
  146.4 3.4 %all-to-all-start.4 = ((f32[4,7,2048]{2,1,0:T(8,128)}), f32[4,7,2048]{2,1,0:T(8,128)S(1)}, u32[]{:S(2)}, u32[]{:S(2)}) async-start(f32[4,7,2048]{2,1,0:T(8,128)} %all_to_all.31), calls=%async_computation.5 | async-start | bytes 524288 | tf_op jit(solution)/shard_map/all_to_all | solution.py:69
  149.9 0.7 all_to_all.28
  150.6 15.6 %all-to-all-done.4 = f32[4,7,2048]{2,1,0:T(8,128)S(1)} async-done(((f32[4,7,2048]{2,1,0:T(8,128)}), f32[4,7,2048]{2,1,0:T(8,128)S(1)}, u32[]{:S(2)}, u32[]{:S(2)}) %all-to-all-start.4) | async-done | bytes 229408 | tf_op jit(solution)/shard_map/all_to_all | solution.py:69
  166.2 3.6 %all-to-all-start.3 = ((f32[4,7,2048]{2,1,0:T(8,128)}), f32[4,7,2048]{2,1,0:T(8,128)S(1)}, u32[]{:S(2)}, u32[]{:S(2)}) async-start(f32[4,7,2048]{2,1,0:T(8,128)} %all_to_all.28), calls=%async_computation.4 | async-start | bytes 524288 | tf_op jit(solution)/shard_map/all_to_all | solution.py:68
  169.9 0.6 gather_fusion.9
  170.5 16.9 %all-to-all-done.3 = f32[4,7,2048]{2,1,0:T(8,128)S(1)} async-done(((f32[4,7,2048]{2,1,0:T(8,128)}), f32[4,7,2048]{2,1,0:T(8,128)S(1)}, u32[]{:S(2)}, u32[]{:S(2)}) %all-to-all-start.3) | async-done | bytes 229408 | tf_op jit(solution)/shard_map/all_to_all | solution.py:68
  187.4 0.6 gather_fusion.7
  188.2 0.5 copy.59
  188.7 0.5 copy-done.6
  189.1 1.1 copy.56
  190.2 1.9 subtract_convert_fusion
  192.1 10.4 %all_gather.3 = bf16[20,16384]{1,0:T(8,128)(2,1)S(1)} all-gather(bf16[20,2048]{1,0:T(8,128)(2,1)S(1)} %get-tuple-element.27), channel_id=1, replica_groups=mesh['dp'=8,'mp'=4] {'dp'}, dimensions={1}, use_global_device_ids=true | all-gather | bytes 737280 | tf_op jit(solution)/shard_map/all_gather | solution.py:148
  202.5 0.2 copy.61
  202.7 0.9 slice.29
  203.6 1.1 convert_element_type.52
  204.7 0.9 copy.57
  (115 shorter events, 2.3 us)
Async XLA Ops:
  8.0 2.4 %copy-start = (bf16[28,128,128]{2,1,0:T(8,128)(2,1)S(1)}, bf16[28,128,128]{2,1,0:T(8,128)(2,1)}, u32[]{:S(2)}) copy-start(bf16[28,128,128]{2,1,0:T(8,128)(2,1)} %param.13) | copy-start | bytes 2752516
  9.4 11.4 %copy-start.26 = (s32[112]{0:T(128)}, s32[112]{0:T(128)S(1)}, u32[]{:S(2)}) copy-start(s32[112]{0:T(128)S(1)} %get-tuple-element.43) | copy-start | bytes 1348
  10.2 2.1 copy-start.30
  10.3 0.8 copy-start.12
  10.4 0.8 copy-start.14
  12.3 6.6 %copy-start.11 = (s32[80,2]{0,1:T(2,128)S(1)}, s32[80,2]{0,1:T(2,128)}, u32[]{:S(2)}) copy-start(s32[80,2]{0,1:T(2,128)} %param.16) | copy-start | bytes 1924
  12.3 12.2 %copy-start.7 = (bf16[128,5120]{1,0:T(8,128)(2,1)S(1)}, bf16[128,5120]{1,0:T(8,128)(2,1)}, u32[]{:S(2)}) copy-start(bf16[128,5120]{1,0:T(8,128)(2,1)} %param.11) | copy-start | bytes 3932164
  12.3 29.5 %all-to-all-start = ((bf16[28,128,128]{2,1,0:T(8,128)(2,1)}), bf16[28,128,128]{2,1,0:T(8,128)(2,1)}, u32[]{:S(2)}, u32[]{:S(2)}) async-start(bf16[28,128,128]{2,1,0:T(8,128)(2,1)} %select_select_fusion.1), calls=%async_computation | async-start | bytes 1835008 | tf_op jit(solution)/shard_map/all_to_all | solution.py:66
  20.9 3.6 %copy-start.18 = (s32[20]{0:T(128)}, s32[20]{0:T(128)S(1)}, u32[]{:S(2)}) copy-start(s32[20]{0:T(128)S(1)} %select_reduce_fusion.3) | copy-start | bytes 244
  22.7 1.9 copy-start.23
  26.1 1.6 copy-start.34
  26.1 1.6 copy-start.16
  26.1 1.6 copy-start.27
  26.2 1.7 copy-start.24
  26.2 1.8 copy-start.19
  27.7 16.9 %copy-start.8 = (bf16[20,128,128]{2,1,0:T(8,128)(2,1)S(1)}, bf16[20,128,128]{2,1,0:T(8,128)(2,1)}, u32[]{:S(2)}) copy-start(bf16[20,128,128]{2,1,0:T(8,128)(2,1)} %gather_fusion) | copy-start | bytes 1966084
  27.9 17.1 %copy-start.20 = (pred[20]{0:T(512)(128)(4,1)}, pred[20]{0:T(512)(128)(4,1)S(1)}, u32[]{:S(2)}) copy-start(pred[20]{0:T(512)(128)(4,1)S(1)} %fusion.31) | copy-start | bytes 64
  28.0 15.7 %copy-start.32 = (pred[20]{0:T(512)(128)(4,1)}, pred[20]{0:T(512)(128)(4,1)S(1)}, u32[]{:S(2)}) copy-start(pred[20]{0:T(512)(128)(4,1)S(1)} %and_bitcast_fusion) | copy-start | bytes 64
  43.7 0.8 copy-start.3
  47.2 37.2 %all-to-all-start.1 = ((bf16[44,128,128]{2,1,0:T(8,128)(2,1)}), bf16[44,128,128]{2,1,0:T(8,128)(2,1)S(1)}, u32[]{:S(2)}, u32[]{:S(2)}) async-start(bf16[44,128,128]{2,1,0:T(8,128)(2,1)} %select_select_fusion), calls=%async_computation.1 | async-start | bytes 2883584 | tf_op jit(solution)/shard_map/all_to_all | solution.py:93
  50.7 1.4 copy-start.28
  50.7 1.4 copy-start.29
  92.7 3.8 %copy-start.25 = (s32[20]{0:T(128)S(1)}, s32[20]{0:T(128)}, u32[]{:S(2)}) copy-start(s32[20]{0:T(128)} %copy-done.23) | copy-start | bytes 244
  92.7 37.4 %all-to-all-start.2 = ((bf16[44,128,128]{2,1,0:T(8,128)(2,1)}), bf16[44,128,128]{2,1,0:T(8,128)(2,1)S(1)}, u32[]{:S(2)}, u32[]{:S(2)}) async-start(bf16[44,128,128]{2,1,0:T(8,128)(2,1)} %copy.53), calls=%async_computation.2 | async-start | bytes 2883584 | tf_op jit(solution)/shard_map/all_to_all | solution.py:117
  96.4 35.2 %copy-start.9 = (bf16[20,128,128]{2,1,0:T(8,128)(2,1)S(1)}, bf16[20,128,128]{2,1,0:T(8,128)(2,1)}, u32[]{:S(2)}) copy-start(bf16[20,128,128]{2,1,0:T(8,128)(2,1)} %gather_fusion) | copy-start | bytes 1966084
  96.4 35.2 %copy-start.22 = (pred[20]{0:T(512)(128)(4,1)S(1)}, pred[20]{0:T(512)(128)(4,1)}, u32[]{:S(2)}) copy-start(pred[20]{0:T(512)(128)(4,1)} %get-tuple-element.30) | copy-start | bytes 64
  96.4 35.2 %copy-start.33 = (pred[20]{0:T(512)(128)(4,1)S(1)}, pred[20]{0:T(512)(128)(4,1)}, u32[]{:S(2)}) copy-start(pred[20]{0:T(512)(128)(4,1)} %copy-done.32) | copy-start | bytes 64
  96.4 93.9 %all-reduce.2.cloned.1.call-start = ((), (), s32[]{:S(2)}) async-start(), calls=%async_computation.7 | async-start | bytes 1572864 | tf_op jit(solution)/shard_map/psum | solution.py:136
  133.2 1.5 copy-start.4
  133.2 1.5 copy-start.10
  133.2 1.5 copy-start.21
  134.7 68.9 %reduce-scatter.2.cloned.1.call-start = ((), (), s32[]{:S(2)}) async-start(), calls=%async_computation.6 | async-start | bytes 3276800 | tf_op jit(solution)/shard_map/reduce_scatter | solution.py:132
  143.3 0.6 copy-start.31
  143.3 1.0 copy-start.1
  143.9 1.0 copy-start.2
  144.9 0.7 copy-start.13
  144.9 0.7 copy-start.15
  145.7 24.1 %copy-start.17 = (s32[20]{0:T(128)S(1)}, s32[20]{0:T(128)}, u32[]{:S(2)}) copy-start(s32[20]{0:T(128)} %get-tuple-element.33) | copy-start | bytes 244
  146.4 19.8 %all-to-all-start.4 = ((f32[4,7,2048]{2,1,0:T(8,128)}), f32[4,7,2048]{2,1,0:T(8,128)S(1)}, u32[]{:S(2)}, u32[]{:S(2)}) async-start(f32[4,7,2048]{2,1,0:T(8,128)} %all_to_all.31), calls=%async_computation.5 | async-start | bytes 524288 | tf_op jit(solution)/shard_map/all_to_all | solution.py:69
  166.2 21.2 %all-to-all-start.3 = ((f32[4,7,2048]{2,1,0:T(8,128)}), f32[4,7,2048]{2,1,0:T(8,128)S(1)}, u32[]{:S(2)}, u32[]{:S(2)}) async-start(f32[4,7,2048]{2,1,0:T(8,128)} %all_to_all.28), calls=%async_computation.4 | async-start | bytes 524288 | tf_op jit(solution)/shard_map/all_to_all | solution.py:68
  170.5 17.6 %copy-start.5 = (bf16[20,128,128]{2,1,0:T(8,128)(2,1)S(1)}, bf16[20,128,128]{2,1,0:T(8,128)(2,1)}, u32[]{:S(2)}) copy-start(bf16[20,128,128]{2,1,0:T(8,128)(2,1)} %copy-done.3) | copy-start | bytes 1966084
  188.1 1.1 copy-start.6
Sparse Core Ops, SparseCore 0:
  134.8 54.8 all-reduce.1
Sparse Core Ops, SparseCore 1:
  143.4 59.5 reduce-scatter.1
where the time goes:
time: 214 us; the launch traced here: 213 us
  waiting for transfers between devices  111 us (52%)
  local copies, waits for them, and re-layouts  28.9 us (14%)
  starting transfers between devices  20.8 us (10%)
  other arithmetic  18.8 us (9%)
  between operations  16.2 us (8%)
  blocking collectives  10.4 us (5%)
  matrix products  6.59 us (3%)
    all_to_all x1, waiting for transfers between devices, body(): lax.all_to_all(outgoing_slopes, 'mp', split_axis=0, concat_axis=0, tiled=...  33.6 us
    all_to_all x1, waiting for transfers between devices, body(): lax.all_to_all(outgoing_products, 'mp', split_axis=0, concat_axis=0, tile...  32 us
    all_to_all x1, waiting for transfers between devices, body(): lax.all_to_all(out_first, 'mp', split_axis=0, concat_axis=0, tiled=True)  16.9 us
    all_to_all x1, waiting for transfers between devices, body(): lax.all_to_all(out_second, 'mp', split_axis=0, concat_axis=0, tiled=True)  15.6 us
    all_to_all x1, waiting for transfers between devices, body(): lax.all_to_all(outgoing, 'mp', split_axis=0, concat_axis=0, tiled=True)  13.3 us
    all_gather x1, blocking collectives, body(): lax.all_gather(weight_next, 'dp', axis=1, tiled=True)  10.4 us
    unnamed x79, local copies, waits for them, and re-layouts  8.8 us
    all_to_all x1, starting transfers between devices, body(): lax.all_to_all(outgoing, 'mp', split_axis=0, concat_axis=0, tiled=True)  6.48 us
  transfers between devices with their start and end apart: 7, of which 5 were waited for; matrix products, arithmetic and copies ran while one was open for 13% of the time, Pallas kernels for 0%

commit v1 on v0

--- a/solution.py
+++ b/solution.py
@@ -8,6 +8,18 @@
 BETA_TWO = 0.95
 LEARN_RATE = 0.01
 ADAM_EPSILON = 0.05
+
+
+def sent_to_each(value, axis, split, join):
+    ways, here = (lax.axis_size(axis), lax.axis_index(axis))
+    width = value.shape[split] // ways
+    turned = jnp.roll(value, -here * width, axis=split)
+    got = [lax.slice_in_dim(turned, 0, width, axis=split)]
+    for far in range(1, ways):
+        sent = lax.slice_in_dim(turned, far * width, (far + 1) * width, axis=split)
+        got.append(lax.ppermute(sent, axis, [(d, (d + far) % ways) for d in range(ways)]))
+    line = jnp.concatenate(got[::-1], axis=join)
+    return jnp.roll(line, (here + 1) * got[0].shape[join], axis=join)
 
 
 def gelu_tanh(values):
@@ -114,7 +126,7 @@
     outgoing_slopes = jnp.einsum(
         "qc,tcn->qtn", placement, band_slopes, preferred_element_type=jnp.float32
     ).astype(jnp.bfloat16)
-    arrived_slopes = lax.all_to_all(outgoing_slopes, "mp", split_axis=0, concat_axis=0, tiled=True)
+    arrived_slopes = sent_to_each(outgoing_slopes, "mp", 0, 0)
     slope_blocks = jnp.take(arrived_slopes, out_place, axis=0)
     slope_form = "btn"
     block_grads = jnp.einsum(

time: 214 us -> 233 us (1.089)
  starting transfers between devices: 20.8 us -> 30 us
  other arithmetic: 18.8 us -> 25.9 us
    ppermute x0 -> x3, waiting for transfers between devices: none -> 33.7 us  [sent_to_each(): lax.ppermute(sent, axis, [(d, (d + far) % ways) for d in range(ways)])]
    all_to_all x1 -> x0, waiting for transfers between devices: 33.6 us -> none  [body(): lax.all_to_all(outgoing_slopes, 'mp', split_axis=0, concat_axis=0, tiled=...]
    all_to_all x1, starting transfers between devices: 3.43 us -> 12.1 us  [body(): lax.all_to_all(out_second, 'mp', split_axis=0, concat_axis=0, tiled=True)]
    concatenate x0 -> x2, other arithmetic: none -> 6.9 us  [the longest x1 5.54 us: sent_to_each(): return jnp.roll(line, (here + 1) * got[0].shape[join], axis=join)]
    ppermute x0 -> x3, starting transfers between devices: none -> 3.83 us  [sent_to_each(): lax.ppermute(sent, axis, [(d, (d + far) % ways) for d in range(ways)])]
    all_to_all x1 -> x0, starting transfers between devices: 3.68 us -> none  [body(): lax.all_to_all(outgoing_slopes, 'mp', split_axis=0, concat_axis=0, tiled=...]
    unnamed x79 -> x77, local copies, waits for them, and re-layouts: 8.8 us -> 8.8 us
  transfers between devices with their start and end apart: 7 -> 9, of which waited for: 5 -> 8; matrix products, arithmetic and copies ran while one was open for 13% -> 12% of each run, Pallas kernels for 0% -> 0%
where the time goes in v1:
time: 233 us; the launch traced here: 232 us
  waiting for transfers between devices  112 us (48%)
  local copies, waits for them, and re-layouts  30.5 us (13%)
  starting transfers between devices  30 us (13%)
  other arithmetic  25.9 us (11%)
  between operations  16.2 us (7%)
  blocking collectives  9.53 us (4%)
  matrix products  7.7 us (3%)
    ppermute x3, waiting for transfers between devices, sent_to_each(): lax.ppermute(sent, axis, [(d, (d + far) % ways) for d in range(ways)])  33.7 us
    all_to_all x1, waiting for transfers between devices, body(): lax.all_to_all(outgoing_products, 'mp', split_axis=0, concat_axis=0, tile...  31.9 us
    all_to_all x1, waiting for transfers between devices, body(): lax.all_to_all(out_second, 'mp', split_axis=0, concat_axis=0, tiled=True)  15.9 us
    all_to_all x1, waiting for transfers between devices, body(): lax.all_to_all(out_first, 'mp', split_axis=0, concat_axis=0, tiled=True)  14.8 us
    all_to_all x1, waiting for transfers between devices, body(): lax.all_to_all(outgoing, 'mp', split_axis=0, concat_axis=0, tiled=True)  13.3 us
    all_to_all x1, starting transfers between devices, body(): lax.all_to_all(out_second, 'mp', split_axis=0, concat_axis=0, tiled=True)  12.1 us
    all_gather x1, blocking collectives, body(): lax.all_gather(weight_next, 'dp', axis=1, tiled=True)  9.53 us
    unnamed x77, local copies, waits for them, and re-layouts  8.8 us
  transfers between devices with their start and end apart: 9, of which 8 were waited for; matrix products, arithmetic and copies ran while one was open for 12% of the time, Pallas kernels for 0%

profile of v1, /device:TPU:0, one launch (start us, length us, event | category | flops | bytes accessed | tf_op | source)
XLA Modules:
  0.0 231.9 jit_solution(16139799399601016081)
XLA Ops:
  8.0 0.7 compare_and_fusion.3
  8.8 0.7 broadcast_subtract_fusion
  10.4 0.7 gather_fusion.2
  11.2 1.2 select_select_fusion.1
  12.3 6.5 %all-to-all-start = ((bf16[28,128,128]{2,1,0:T(8,128)(2,1)}), bf16[28,128,128]{2,1,0:T(8,128)(2,1)}, u32[]{:S(2)}, u32[]{:S(2)}) async-start(bf16[28,128,128]{2,1,0:T(8,128)(2,1)} %select_select_fusion.1), calls=%async_computation | async-start | bytes 1835008 | tf_op jit(solution)/shard_map/all_to_all | solution.py:78
  19.1 0.5 broadcast.538
  19.6 1.2 fusion.59
  21.5 0.5 compare_select_fusion.10
  22.0 0.6 compare_and_fusion
  22.6 0.6 select_reduce_fusion.4
  23.3 0.7 gather_fusion.1
  24.0 0.5 fusion.48
  24.5 0.8 copy.47
  25.3 0.8 copy.48
  26.2 1.5 gather_fusion
  28.0 0.6 compare_and_fusion.2
  28.6 13.3 %all-to-all-done = bf16[28,128,128]{2,1,0:T(8,128)(2,1)} async-done(((bf16[28,128,128]{2,1,0:T(8,128)(2,1)}), bf16[28,128,128]{2,1,0:T(8,128)(2,1)}, u32[]{:S(2)}, u32[]{:S(2)}) %all-to-all-start) | async-done | bytes 917536 | tf_op jit(solution)/shard_map/all_to_all | solution.py:78
  41.8 1.8 gather_fusion.3
  43.7 0.8 copy-done.3
  44.5 1.5 convolution_convert_fusion.2
  46.1 0.8 gather_fusion.4
  46.9 1.4 select_select_fusion
  48.3 3.7 %all-to-all-start.1 = ((bf16[44,128,128]{2,1,0:T(8,128)(2,1)}), bf16[44,128,128]{2,1,0:T(8,128)(2,1)S(1)}, u32[]{:S(2)}, u32[]{:S(2)}) async-start(bf16[44,128,128]{2,1,0:T(8,128)(2,1)} %select_select_fusion), calls=%async_computation.1 | async-start | bytes 2883584 | tf_op jit(solution)/shard_map/all_to_all | solution.py:105
  52.0 1.4 copy.51
  53.7 31.9 %all-to-all-done.1 = bf16[44,128,128]{2,1,0:T(8,128)(2,1)S(1)} async-done(((bf16[44,128,128]{2,1,0:T(8,128)(2,1)}), bf16[44,128,128]{2,1,0:T(8,128)(2,1)S(1)}, u32[]{:S(2)}, u32[]{:S(2)}) %all-to-all-start.1) | async-done | bytes 1441824 | tf_op jit(solution)/shard_map/all_to_all | solution.py:105
  85.6 2.1 fusion.10
  87.7 1.8 copy.50
  89.5 2.1 fusion.15
  91.6 1.5 copy.52
  93.1 0.6 convolution_convert_fusion
  93.7 1.4 fusion.7
  95.1 1.6 fusion.60
  96.7 2.0 collective-permute-start.1
  98.7 1.8 collective-permute-start
  100.5 13.1 %collective-permute-done.2 = bf16[11,128,128]{2,0,1:T(8,128)(2,1)S(1)} collective-permute-done((bf16[11,128,128]{2,0,1:T(8,128)(2,1)}, bf16[11,128,128]{2,0,1:T(8,128)(2,1)S(1)}, u32[]{:S(2)}, u32[]{:S(2)}) %collective-permute-start.2) | collective-permute-done | bytes 360480 | tf_op jit(solution)/shard_map/ppermute | solution.py:20
  113.6 20.6 %collective-permute-done.1 = bf16[11,128,128]{2,0,1:T(8,128)(2,1)S(1)} collective-permute-done((bf16[11,128,128]{2,0,1:T(8,128)(2,1)}, bf16[11,128,128]{2,0,1:T(8,128)(2,1)S(1)}, u32[]{:S(2)}, u32[]{:S(2)}) %collective-permute-start.1) | collective-permute-done | bytes 360480 | tf_op jit(solution)/shard_map/ppermute | solution.py:20
  134.2 5.5 %fusion.3 = bf16[44,128,128]{2,0,1:T(8,128)(2,1)S(1)} fusion(s32[]{:T(128)S(6)} %select_n.302, bf16[11,128,128]{2,0,1:T(8,128)(2,1)S(1)} %collective-permute-done, bf16[11,128,128]{2,0,1:T(8,128)(2,1)S(1)} %collective-permute-done.1, bf16[11,128,128]{2,0,1:T(8,128)(2,1)S(1)} %collective-permute-done.2, bf16[11,128,128]{2,0,1:T(8,128)(2,1)S(1)} %get-tuple-element.39), kind=kLoop, calls=%fused_computation.29 | loop fusion | flops 11534336 | bytes 2883588 | tf_op jit(solution)/shard_map/jit(_roll_dynamic)/concatenate | solution.py:22
  140.2 1.5 gather_fusion.5
  141.7 1.6 convolution_convert_fusion.1
  143.4 1.4 copy.60
  144.9 1.7 fusion.27
  146.9 4.4 %scatter_fusion = f32[128,40,128]{2,0,1:T(8,128)S(1)} fusion(f32[128,40,128]{2,0,1:T(8,128)S(1)} %broadcast_in_dim.224, s32[20]{0:T(128)S(1)} %get-tuple-element.53, f32[20,128,128]{2,1,0:T(8,128)} %fusion.27), kind=kCustom, calls=%fused_computation.10 | custom fusion | flops 327680 | bytes 3932240 | tf_op jit(solution)/shard_map/scatter-add | solution.py:142
  151.3 2.1 copy.54
  153.5 0.6 copy-done.30
  154.4 0.6 gather_fusion.8
  155.1 0.6 gather_fusion.6
  155.9 0.7 all_to_all.27
  156.6 12.1 %all-to-all-start.3 = ((f32[4,7,2048]{2,1,0:T(8,128)}), f32[4,7,2048]{2,1,0:T(8,128)S(1)}, u32[]{:S(2)}, u32[]{:S(2)}) async-start(f32[4,7,2048]{2,1,0:T(8,128)} %all_to_all.27), calls=%async_computation.4 | async-start | bytes 524288 | tf_op jit(solution)/shard_map/all_to_all | solution.py:81
  168.7 0.7 all_to_all.24
  169.4 15.9 %all-to-all-done.3 = f32[4,7,2048]{2,1,0:T(8,128)S(1)} async-done(((f32[4,7,2048]{2,1,0:T(8,128)}), f32[4,7,2048]{2,1,0:T(8,128)S(1)}, u32[]{:S(2)}, u32[]{:S(2)}) %all-to-all-start.3) | async-done | bytes 229408 | tf_op jit(solution)/shard_map/all_to_all | solution.py:81
  185.3 3.8 %all-to-all-start.2 = ((f32[4,7,2048]{2,1,0:T(8,128)}), f32[4,7,2048]{2,1,0:T(8,128)S(1)}, u32[]{:S(2)}, u32[]{:S(2)}) async-start(f32[4,7,2048]{2,1,0:T(8,128)} %all_to_all.24), calls=%async_computation.3 | async-start | bytes 524288 | tf_op jit(solution)/shard_map/all_to_all | solution.py:80
  189.2 0.6 gather_fusion.9
  189.9 14.8 %all-to-all-done.2 = f32[4,7,2048]{2,1,0:T(8,128)S(1)} async-done(((f32[4,7,2048]{2,1,0:T(8,128)}), f32[4,7,2048]{2,1,0:T(8,128)S(1)}, u32[]{:S(2)}, u32[]{:S(2)}) %all-to-all-start.2) | async-done | bytes 229408 | tf_op jit(solution)/shard_map/all_to_all | solution.py:80
  204.7 0.6 gather_fusion.7
  205.4 0.5 copy.59
  205.9 0.5 copy-done.6
  206.4 1.1 copy.56
  207.5 1.7 all-reduce.2.cloned.1.call-done
  209.2 1.9 subtract_convert_fusion
  211.1 9.5 %all_gather.3 = bf16[20,16384]{1,0:T(8,128)(2,1)S(1)} all-gather(bf16[20,2048]{1,0:T(8,128)(2,1)S(1)} %get-tuple-element.28), channel_id=1, replica_groups=mesh['dp'=8,'mp'=4] {'dp'}, dimensions={1}, use_global_device_ids=true | all-gather | bytes 737280 | tf_op jit(solution)/shard_map/all_gather | solution.py:160
  220.8 0.9 slice.49
  221.7 0.8 reduce-scatter.2.cloned.1.call-done
  222.4 1.1 convert_element_type.52
  223.5 0.9 copy.57
  (120 shorter events, 4.1 us)
Async XLA Ops:
  8.0 2.4 %copy-start = (bf16[28,128,128]{2,1,0:T(8,128)(2,1)S(1)}, bf16[28,128,128]{2,1,0:T(8,128)(2,1)}, u32[]{:S(2)}) copy-start(bf16[28,128,128]{2,1,0:T(8,128)(2,1)} %param.15) | copy-start | bytes 2752516
  9.4 11.3 %copy-start.26 = (s32[112]{0:T(128)}, s32[112]{0:T(128)S(1)}, u32[]{:S(2)}) copy-start(s32[112]{0:T(128)S(1)} %get-tuple-element.48) | copy-start | bytes 1348
  10.2 0.9 copy-start.29
  10.3 2.0 copy-start.11
  10.4 2.0 copy-start.13
  11.1 7.8 %copy-start.10 = (s32[80,2]{0,1:T(2,128)S(1)}, s32[80,2]{0,1:T(2,128)}, u32[]{:S(2)}) copy-start(s32[80,2]{0,1:T(2,128)} %param.18) | copy-start | bytes 1924
  12.3 12.2 %copy-start.7 = (bf16[128,5120]{1,0:T(8,128)(2,1)S(1)}, bf16[128,5120]{1,0:T(8,128)(2,1)}, u32[]{:S(2)}) copy-start(bf16[128,5120]{1,0:T(8,128)(2,1)} %param.13) | copy-start | bytes 3932164
  12.3 29.5 %all-to-all-start = ((bf16[28,128,128]{2,1,0:T(8,128)(2,1)}), bf16[28,128,128]{2,1,0:T(8,128)(2,1)}, u32[]{:S(2)}, u32[]{:S(2)}) async-start(bf16[28,128,128]{2,1,0:T(8,128)(2,1)} %select_select_fusion.1), calls=%async_computation | async-start | bytes 1835008 | tf_op jit(solution)/shard_map/all_to_all | solution.py:78
  20.9 3.6 %copy-start.17 = (s32[20]{0:T(128)}, s32[20]{0:T(128)S(1)}, u32[]{:S(2)}) copy-start(s32[20]{0:T(128)S(1)} %select_reduce_fusion.3) | copy-start | bytes 244
  22.6 1.9 copy-start.22
  26.1 1.6 copy-start.33
  26.1 1.6 copy-start.15
  26.1 1.6 copy-start.27
  26.1 1.7 copy-start.23
  26.1 1.8 copy-start.18
  27.8 18.2 %copy-start.19 = (pred[20]{0:T(512)(128)(4,1)}, pred[20]{0:T(512)(128)(4,1)S(1)}, u32[]{:S(2)}) copy-start(pred[20]{0:T(512)(128)(4,1)S(1)} %fusion.39) | copy-start | bytes 64
  28.0 18.1 %copy-start.31 = (pred[20]{0:T(512)(128)(4,1)}, pred[20]{0:T(512)(128)(4,1)S(1)}, u32[]{:S(2)}) copy-start(pred[20]{0:T(512)(128)(4,1)S(1)} %and_bitcast_fusion) | copy-start | bytes 64
  43.7 0.8 copy-start.3
  48.3 5.2 %copy-start.25 = (s32[80]{0:T(128)S(1)}, s32[80]{0:T(128)}, u32[]{:S(2)}) copy-start(s32[80]{0:T(128)} %get-tuple-element.47) | copy-start | bytes 964
  48.3 5.2 %copy-start.28 = (s32[80]{0:T(128)S(1)}, s32[80]{0:T(128)}, u32[]{:S(2)}) copy-start(s32[80]{0:T(128)} %get-tuple-element.35) | copy-start | bytes 964
  48.3 37.4 %all-to-all-start.1 = ((bf16[44,128,128]{2,1,0:T(8,128)(2,1)}), bf16[44,128,128]{2,1,0:T(8,128)(2,1)S(1)}, u32[]{:S(2)}, u32[]{:S(2)}) async-start(bf16[44,128,128]{2,1,0:T(8,128)(2,1)} %select_select_fusion), calls=%async_computation.1 | async-start | bytes 2883584 | tf_op jit(solution)/shard_map/all_to_all | solution.py:105
  51.9 157.2 %all-reduce.2.cloned.1.call-start = ((), (), s32[]{:S(2)}) async-start(), calls=%async_computation.6 | async-start | bytes 1572864 | tf_op jit(solution)/shard_map/psum | solution.py:148
  95.1 5.5 %copy-start.24 = (s32[20]{0:T(128)S(1)}, s32[20]{0:T(128)}, u32[]{:S(2)}) copy-start(s32[20]{0:T(128)} %copy-done.22) | copy-start | bytes 244
  96.7 16.9 %collective-permute-start.2 = (bf16[11,128,128]{2,0,1:T(8,128)(2,1)}, bf16[11,128,128]{2,0,1:T(8,128)(2,1)S(1)}, u32[]{:S(2)}, u32[]{:S(2)}) collective-permute-start(bf16[11,128,128]{2,0,1:T(8,128)(2,1)} %get-tuple-element.40), channel_id=1, source_target_pairs={{0,1},{1,2},{2,3},{3,0},{4,5},{5,6},{6,7},{7,4},{8,9},{9,10},{10,1... | collective-permute-start | bytes 1081352 | tf_op jit(solution)/shard_map/ppermute | solution.py:20
  96.7 37.6 %collective-permute-start.1 = (bf16[11,128,128]{2,0,1:T(8,128)(2,1)}, bf16[11,128,128]{2,0,1:T(8,128)(2,1)S(1)}, u32[]{:S(2)}, u32[]{:S(2)}) collective-permute-start(bf16[11,128,128]{2,0,1:T(8,128)(2,1)} %get-tuple-element.41), channel_id=1, source_target_pairs={{0,2},{1,3},{2,0},{3,1},{4,6},{5,7},{6,4},{7,5},{8,10},{9,11},{10,... | collective-permute-start | bytes 1081352 | tf_op jit(solution)/shard_map/ppermute | solution.py:20
  98.7 35.5 %collective-permute-start = (bf16[11,128,128]{2,0,1:T(8,128)(2,1)S(1)}, bf16[11,128,128]{2,0,1:T(8,128)(2,1)S(1)}, u32[]{:S(2)}, u32[]{:S(2)}) collective-permute-start(bf16[11,128,128]{2,0,1:T(8,128)(2,1)S(1)} %get-tuple-element.42), channel_id=1, source_target_pairs={{0,3},{1,0},{2,1},{3,2},{4,7},{5,4},{6,5},{7,6},{8,11},{9,8},{10,9... | collective-permute-start | bytes 1081352 | tf_op jit(solution)/shard_map/ppermute | solution.py:20
  139.8 1.9 copy-start.8
  139.8 1.9 copy-start.21
  139.8 1.9 copy-start.32
  143.3 1.6 copy-start.4
  143.3 1.6 copy-start.9
  143.3 1.6 copy-start.20
  144.8 77.6 %reduce-scatter.2.cloned.1.call-start = ((), (), s32[]{:S(2)}) async-start(), calls=%async_computation.5 | async-start | bytes 3276800 | tf_op jit(solution)/shard_map/reduce_scatter | solution.py:144
  153.4 0.6 copy-start.30
  153.4 1.0 copy-start.1
  154.1 1.0 copy-start.2
  155.1 0.7 copy-start.12
  155.1 0.7 copy-start.14
  155.7 33.4 %copy-start.16 = (s32[20]{0:T(128)S(1)}, s32[20]{0:T(128)}, u32[]{:S(2)}) copy-start(s32[20]{0:T(128)} %get-tuple-element.34) | copy-start | bytes 244
  156.6 28.7 %all-to-all-start.3 = ((f32[4,7,2048]{2,1,0:T(8,128)}), f32[4,7,2048]{2,1,0:T(8,128)S(1)}, u32[]{:S(2)}, u32[]{:S(2)}) async-start(f32[4,7,2048]{2,1,0:T(8,128)} %all_to_all.27), calls=%async_computation.4 | async-start | bytes 524288 | tf_op jit(solution)/shard_map/all_to_all | solution.py:81
  185.3 19.3 %all-to-all-start.2 = ((f32[4,7,2048]{2,1,0:T(8,128)}), f32[4,7,2048]{2,1,0:T(8,128)S(1)}, u32[]{:S(2)}, u32[]{:S(2)}) async-start(f32[4,7,2048]{2,1,0:T(8,128)} %all_to_all.24), calls=%async_computation.3 | async-start | bytes 524288 | tf_op jit(solution)/shard_map/all_to_all | solution.py:80
  189.8 15.4 %copy-start.5 = (bf16[20,128,128]{2,1,0:T(8,128)(2,1)S(1)}, bf16[20,128,128]{2,1,0:T(8,128)(2,1)}, u32[]{:S(2)}) copy-start(bf16[20,128,128]{2,1,0:T(8,128)(2,1)} %copy-done.3) | copy-start | bytes 1966084
  205.3 1.1 copy-start.6
Sparse Core Ops, SparseCore 0:
  144.9 64.1 all-reduce.1
Sparse Core Ops, SparseCore 1:
  153.6 68.8 reduce-scatter.1
